TPU v7x, 32 devices: a whole 2x2x4 slice. The times are simulated.
32 devices in a mesh: wide: 16 (over z, y, core), shift: 2 (over x).
Axes of the slice: x: 2, y: 2, z: 4, core: 2. Of those that a mesh axis runs over, the one named last changes fastest.
Arguments:
- particles: bfloat16 [1024, 8448], P('wide'), may hold values from -64 to 64
- group_id: int32 [1024, 1], P('wide'), may hold values from 0 to 15; in each aligned block of 64 rows (0 to 63, 64 to 127, ...) at most 8 rows name the same one
- ctf_curves: float32 [16, 4224], P('wide'), may hold values from -1 to 1
- projections: bfloat16 [16, 8448], P('wide')
- inv_noise: float32 [4224], replicated, may hold values from 0.5 to 2
- shifts: int32 [64, 2], P('shift'), may hold values from -8 to 8
Outputs:
- insertion: float32 [16, 12672], P('wide')
- log_evidence: float32 [1024], P('wide')
Inputs may be any that keep to these rules, and one draw needn't show every extreme that they name: `group_id`: at most 8 of the rows of one device name the same group, a bound that some block reaches.
All inputs are finite; a program needn't handle non-finite values.
Results may differ from a plain program's by a relative error of at most 0.0029.
Values may be sent and summed in bfloat16 or wider, within the bound.
A program may use at most 64 MiB of HBM per device.

v0:
```python
import functools
import math

import jax
import jax.numpy as jnp
from jax import lax
from jax.experimental import pallas as pl
from jax.experimental.pallas import tpu as pltpu
from jax.sharding import PartitionSpec as P

LANE = 128
STEP = 2.0 * math.pi / 128.0
HIGH = lax.Precision.HIGHEST
MESH = pl.DeviceIdType.MESH
F32 = jnp.float32
BF16 = jnp.bfloat16
NT_DIMS = (((1,), (1,)), ((), ()))
NN_DIMS = (((1,), (0,)), ((), ()))
TN_DIMS = (((0,), (0,)), ((), ()))


def dot(a, b, dims=NN_DIMS, precision=None):
    return lax.dot_general(a, b, dims, precision=precision, preferred_element_type=F32)


def kernel(
    cfg, x_hbm, gid_ref, ctf_ref, proj_ref, noise_ref, sh_ref,
    out_ref, ev_ref,
    xbuf, cbuf, pbuf, shbuf, prow, nbuf, cos_t, sin_t, wgt, fil, wsq, power, selfc, selfr, selft, rowbuf,
    sc, scr, tot, wts, wsum, part, r1, r2, fin, fbuf,
    x_sem, own_sem, ag_ssem, ag_rsem, rl_ssem, sh_ssem, sh_rsem,
    sc_ssem, sc_rsem, r1_ssem, r1_rsem, r2_ssem, r2_rsem, f_ssem, f_rsem,
):
    W, S, nl, L, NTL, R = cfg
    C = L * LANE
    NT = NTL * S
    H = W // 2
    NC = W // 2
    QB = 2
    NB = H // QB
    RB = QB * NT
    w = lax.axis_index("wide")
    s = lax.axis_index("shift")
    core = lax.rem(w, 2)
    chip = lax.div(w, 2)
    mate = chip * 2 + (1 - core)
    first = jnp.minimum(s * L, nl - L)
    start = pl.multiple_of(first * LANE, LANE)
    full = nl * LANE
    window = pl.ds(start, C)

    def chip_at(k):
        return lax.rem(chip + k, NC)

    def remote(src, dst, ssem, rsem, wide=None, shift=None):
        return pltpu.make_async_remote_copy(
            src_ref=src, dst_ref=dst, send_sem=ssem, recv_sem=rsem,
            device_id=(w if wide is None else wide, s if shift is None else shift),
            device_id_type=MESH,
        )

    x_copies = [
        pltpu.make_async_copy(
            x_hbm.at[:, pl.ds(pl.multiple_of(start + h * full, LANE), C)],
            xbuf.at[h], x_sem.at[h],
        )
        for h in range(2)
    ]
    own = [
        pltpu.make_async_copy(ctf_ref.at[:, window], cbuf.at[w], own_sem.at[0]),
        pltpu.make_async_copy(proj_ref, prow, own_sem.at[1]),
        pltpu.make_async_copy(sh_ref, shbuf.at[s], own_sem.at[2]),
        pltpu.make_async_copy(noise_ref, nbuf.at[0], own_sem.at[3]),
    ]
    for c in own + x_copies:
        c.start()

    bar = pltpu.get_barrier_semaphore()
    pl.semaphore_signal(bar, inc=1, device_id=(mate, s), device_id_type=MESH)

    def greet(k, carry):
        pl.semaphore_signal(
            bar, inc=1, device_id=(chip_at(k) * 2 + core, s), device_id_type=MESH
        )
        return carry

    lax.fori_loop(1, NC, greet, 0)
    for d in range(1, S):
        pl.semaphore_signal(
            bar, inc=1, device_id=(w, lax.rem(s + d, S)), device_id_type=MESH
        )
    own[1].wait()
    for h in range(2):
        pbuf[w, h : h + 1, :] = prow[:, pl.ds(pl.multiple_of(start + h * full, LANE), C)]

    pl.semaphore_wait(bar, NC + S - 1)

    def ag_pair(k, to):
        return (
            remote(ctf_ref.at[:, window], cbuf.at[w], ag_ssem.at[0, k], ag_rsem.at[0, w], wide=to),
            remote(pbuf.at[w], pbuf.at[w], ag_ssem.at[1, k], ag_rsem.at[1, w], wide=to),
        )

    def relay_pair(src):
        return (
            remote(cbuf.at[src], cbuf.at[src], rl_ssem.at[0, src], ag_rsem.at[0, src], wide=mate),
            remote(pbuf.at[src], pbuf.at[src], rl_ssem.at[1, src], ag_rsem.at[1, src], wide=mate),
        )

    sh_copies = [
        remote(sh_ref, shbuf.at[s], sh_ssem.at[d - 1], sh_rsem.at[s], shift=lax.rem(s + d, S))
        for d in range(1, S)
    ]
    for c in sh_copies:
        c.start()

    def ag_start(k, carry):
        for c in ag_pair(k, chip_at(k) * 2 + core):
            c.start()
        return carry

    lax.fori_loop(1, NC, ag_start, 0)
    for c in ag_pair(0, mate):
        c.start()

    for c in own[:1] + own[2:]:
        c.wait()
    for d in range(1, S):
        other = lax.rem(s + d, S)
        remote(sh_ref, shbuf.at[other], sh_ssem.at[d - 1], sh_rsem.at[other], shift=other).wait_recv()

    lane = lax.broadcasted_iota(jnp.int32, (2, 2 * LANE), 1)
    axis = lax.broadcasted_iota(jnp.int32, (2, 2 * LANE), 0)
    freq = jnp.where(
        lane < LANE, jnp.where(axis == 0, first + lane, 0), jnp.where(axis == 1, lane - LANE - 64, 0)
    ).astype(F32)
    ang = STEP * jnp.concatenate(
        [dot(shbuf[t].astype(F32), freq, TN_DIMS, HIGH) for t in range(S)], axis=0
    )
    ang_a, ang_b = ang[:, :LANE], ang[:, LANE:]
    kx = first + lax.broadcasted_iota(jnp.int32, (NT, LANE), 1)
    live = jnp.where(kx >= s * L, 1.0, 0.0)
    cos_b, sin_b = jnp.cos(ang_b), jnp.sin(ang_b)
    cos_a, sin_a = jnp.cos(ang_a) * live, jnp.sin(ang_a) * live
    for l in range(L):
        ca, sa = cos_a[:, l : l + 1], sin_a[:, l : l + 1]
        cols = pl.ds(l * LANE, LANE)
        cos_t[:, cols] = ca * cos_b - sa * sin_b
        sin_t[:, cols] = sa * cos_b + ca * sin_b

    def relay(k, carry):
        src = lax.rem(chip + NC - k, NC) * 2 + core
        for c in relay_pair(src):
            c.wait_recv()
            c.start()
        return carry

    lax.fori_loop(1, NC, relay, 0)

    def landed(j, carry):
        for c in relay_pair(j * 2 + (1 - core)):
            c.wait_recv()
        return carry

    lax.fori_loop(0, NC, landed, 0)
    for c in x_copies:
        c.wait()

    onehot = jnp.where(
        gid_ref[...] == lax.broadcasted_iota(jnp.int32, (part.shape[2] - C, R), 0), 1.0, 0.0
    )
    pick = onehot[:W]
    for l in range(L):
        cols = pl.ds(l * LANE, LANE)
        curves = cbuf[:, 0, cols]
        row = dot(pick, curves, TN_DIMS, HIGH)
        noise = nbuf[:, pl.ds(pl.multiple_of(start + l * LANE, LANE), LANE)]
        x_re = xbuf[0, :, cols].astype(F32)
        x_im = xbuf[1, :, cols].astype(F32)
        gain = noise * row
        re, im = pl.ds(2 * l * LANE, LANE), pl.ds((2 * l + 1) * LANE, LANE)
        wgt[:, re] = (gain * x_re).astype(BF16)
        wgt[:, im] = (gain * x_im).astype(BF16)
        rowbuf[:, cols] = row

    def sc_copy(b, d):
        rows = pl.ds(pl.multiple_of(b * RB, RB), RB)
        return remote(
            sc.at[rows], scr.at[d - 1, rows], sc_ssem.at[d - 1, b], sc_rsem.at[d - 1, b],
            shift=lax.rem(s + d, S),
        )

    def score_block(b, carry):
        acc = jnp.zeros((2 * RB, R), F32)
        for l in range(L):
            cols = pl.ds(l * LANE, LANE)
            ct, st = cos_t[:, cols], sin_t[:, cols]
            rots = []
            for h in range(2):
                for q in range(QB):
                    o = h * H + b * QB + q
                    pair = pbuf[o, :, cols].astype(F32)
                    pr, pi = pair[0:1], pair[1:2]
                    rots.append(
                        jnp.concatenate(
                            [(pr * ct + pi * st).astype(BF16), (pi * ct - pr * st).astype(BF16)],
                            axis=1,
                        )
                    )
            rot = jnp.concatenate(rots, axis=0)
            acc = acc + dot(rot, wgt[:, pl.ds(2 * l * LANE, 2 * LANE)], NT_DIMS)
        both = jnp.concatenate([acc[:RB], acc[RB:]], axis=1)
        sc[pl.ds(pl.multiple_of(b * RB, RB), RB), :] = both
        for d in range(1, S):
            sc_copy(b, d).start()
        return carry

    lax.fori_loop(0, NB, score_block, 0)

    def square(o, carry):
        p = pbuf[o].astype(F32)
        power[pl.ds(o, 1), :] = jnp.sum(p * p, axis=0, keepdims=True)
        return carry

    lax.fori_loop(0, W, square, 0)
    for l in range(L):
        cols = pl.ds(l * LANE, LANE)
        curves = cbuf[:, 0, cols]
        noise = nbuf[:, pl.ds(pl.multiple_of(start + l * LANE, LANE), LANE)]
        here = jnp.where(first + l >= s * L, 0.5, 0.0)
        wsq[:, cols] = curves * curves * noise * here
    self_g = dot(power[...], wsq[...], NT_DIMS, HIGH)
    self_i = dot(self_g, pick, NN_DIMS, HIGH)
    selfc[...] = jnp.concatenate([self_i[:H], self_i[H:]], axis=1)

    def self_copy(d):
        return remote(
            selfc, selfr.at[d - 1], sc_ssem.at[d - 1, NB], sc_rsem.at[d - 1, NB],
            shift=lax.rem(s + d, S),
        )

    for d in range(1, S):
        self_copy(d).start()
    for l in range(L):
        cols = pl.ds(l * LANE, LANE)
        row = rowbuf[:, cols]
        fil[:, pl.ds(2 * l * LANE, LANE)] = (row * xbuf[0, :, cols].astype(F32)).astype(BF16)
        fil[:, pl.ds((2 * l + 1) * LANE, LANE)] = (row * xbuf[1, :, cols].astype(F32)).astype(BF16)
    self_all = selfc[...]
    for d in range(1, S):
        self_copy(d).wait_recv()
        self_all = self_all + selfr[d - 1]
    selft[...] = self_all

    def swap(v):
        return pltpu.roll(v, R, 1)

    def join(b, m):
        rows = pl.ds(pl.multiple_of(b * RB, RB), RB)
        v = sc[rows, :]
        for d in range(1, S):
            sc_copy(b, d).wait_recv()
            v = v + scr[d - 1, rows, :]
        for q in range(QB):
            u = v[q * NT : (q + 1) * NT] - selft[pl.ds(b * QB + q, 1), :]
            tot[pl.ds(pl.multiple_of(b * RB + q * NT, NT), NT), :] = u
            m = jnp.maximum(m, jnp.max(u.reshape(NT // 8, 8, 2 * R), axis=0))
        return m

    m8 = lax.fori_loop(0, NB, join, jnp.full((8, 2 * R), -jnp.inf, F32))
    top = jnp.max(m8, axis=0, keepdims=True)
    top = jnp.maximum(top, swap(top))

    def expo(b, t):
        rows = pl.ds(pl.multiple_of(b * RB, RB), RB)
        e = jnp.exp(tot[rows, :] - top)
        tot[rows, :] = e
        return t + jnp.sum(e.reshape(RB // 8, 8, 2 * R), axis=0)

    t8 = lax.fori_loop(0, NB, expo, jnp.zeros((8, 2 * R), F32))
    total = jnp.sum(t8, axis=0, keepdims=True)
    total = total + swap(total)
    ev_ref[...] = (top + jnp.log(total))[:, :R]

    def norm(o, carry):
        rows = pl.ds(pl.multiple_of(o * NT, NT), NT)
        v = (tot[rows, :] / total).astype(BF16)
        wts[0, rows, :] = v[:, :R]
        wts[1, rows, :] = v[:, R:]
        wsum[pl.ds(o, 1), :] = jnp.sum(v.astype(F32), axis=0, keepdims=True)
        return carry

    lax.fori_loop(0, H, norm, 0)

    loads = wsum[...]
    extra = pl.ds(C, part.shape[2] - C)
    for h in range(2):
        load = dot(loads[:, h * R : (h + 1) * R], onehot, NT_DIMS, HIGH)
        for o in range(H):
            part[h * H + o, 0:1, extra] = load[o : o + 1]
            part[h * H + o, 1:2, extra] = jnp.zeros_like(load[o : o + 1])

    def r1_copy(j):
        return remote(part.at[2 * j + (1 - core)], r1.at[j], r1_ssem.at[j], r1_rsem.at[j], wide=mate)

    def r2_copy(k):
        to = chip_at(k)
        return remote(
            part.at[2 * to + core], r2.at[k], r2_ssem.at[k], r2_rsem.at[k], wide=2 * to + core
        )

    def update_chip(j):
        h = lax.div(2 * j, H)
        rows = pl.ds(pl.multiple_of(lax.rem(2 * j, H) * NT, 2 * NT), 2 * NT)
        pair = wts[h, rows, :]
        for l in range(L):
            cols = pl.ds(l * LANE, LANE)
            ct, st = cos_t[:, cols], sin_t[:, cols]
            u = dot(pair, fil[:, pl.ds(2 * l * LANE, 2 * LANE)])
            for q in range(2):
                ur = u[q * NT : (q + 1) * NT, :LANE]
                ui = u[q * NT : (q + 1) * NT, LANE:]
                part[2 * j + q, 0:1, cols] = jnp.sum(ur * ct - ui * st, axis=0, keepdims=True)
                part[2 * j + q, 1:2, cols] = jnp.sum(ur * st + ui * ct, axis=0, keepdims=True)

    def r1_take(k):
        j = chip_at(k)
        r1_copy(j).wait_recv()
        part[2 * j + core] = part[2 * j + core] + r1[j]
        r2_copy(k).start()

    def update_step(k, carry):
        j = chip_at(k)
        update_chip(j)
        r1_copy(j).start()

        @pl.when(jnp.logical_and(k >= 2, k <= NC))
        def _():
            r1_take(k - 1)

        return carry

    lax.fori_loop(1, NC + 1, update_step, 0)
    r1_copy(chip).wait_recv()
    fin[...] = part[w] + r1[chip]

    def r2_take(k, carry):
        r2_copy(k).wait_recv()
        fin[...] = fin[...] + r2[k]
        return carry

    lax.fori_loop(1, NC, r2_take, 0)

    load = fin[0:1, C : C + W]
    curves = cbuf[:, 0, :]
    fbuf[s, 0:2, :] = fin[:, :C]
    fbuf[s, 2:3, :] = dot(load, curves * curves, precision=HIGH)

    def f_copy(d):
        return remote(
            fbuf.at[s], fbuf.at[s], f_ssem.at[d - 1], f_rsem.at[s], shift=lax.rem(s + d, S)
        )

    for d in range(1, S):
        f_copy(d).start()
    for d in range(1, S):
        other = lax.rem(s + d, S)
        remote(fbuf.at[other], fbuf.at[other], f_ssem.at[d - 1], f_rsem.at[other], shift=other).wait_recv()
    for t in range(S):
        lo, hi = t * L, min(t * L + L, nl)
        if lo < hi:
            off = lo - min(lo, nl - L)
            for r in range(3):
                out_ref[r : r + 1, lo * LANE : hi * LANE] = fbuf[
                    t, r : r + 1, off * LANE : (off + hi - lo) * LANE
                ]

    for c in sh_copies:
        c.wait_send()
    for c in ag_pair(0, mate):
        c.wait_send()
    r1_copy(chip).wait_send()

    def drain(k, carry):
        for c in ag_pair(k, chip_at(k) * 2 + core):
            c.wait_send()
        for c in relay_pair(lax.rem(chip + NC - k, NC) * 2 + core):
            c.wait_send()
        r1_copy(chip_at(k)).wait_send()
        r2_copy(k).wait_send()
        return carry

    lax.fori_loop(1, NC, drain, 0)

    def drain_sc(b, carry):
        for d in range(1, S):
            sc_copy(b, d).wait_send()
        return carry

    lax.fori_loop(0, NB, drain_sc, 0)
    for d in range(1, S):
        f_copy(d).wait_send()
        self_copy(d).wait_send()


def unfold(rows_ref, ev_in, out_ref, ev_ref):
    n = rows_ref.shape[1]
    for r in range(3):
        out_ref[:, r * n : (r + 1) * n] = rows_ref[r : r + 1, :]
    ev_ref[...] = ev_in[...]


def local(W, S, particles, group_id, ctf_curves, projections, inv_noise, shifts):
    R = particles.shape[0]
    coeffs = inv_noise.shape[0]
    nl = coeffs // LANE
    L = -(-nl // S)
    C = L * LANE
    NTL = shifts.shape[0]
    NT = NTL * S
    H = W // 2
    NB = H // 2
    G = -(-W // LANE) * LANE
    rows = H * NT
    any_spec = pl.BlockSpec(memory_space=pl.ANY)
    vm = pl.BlockSpec(memory_space=pltpu.VMEM)
    dma = pltpu.SemaphoreType.DMA
    V = pltpu.VMEM
    out, ev = pl.pallas_call(
        functools.partial(kernel, (W, S, nl, L, NTL, R)),
        out_shape=(
            jax.ShapeDtypeStruct((3, coeffs), F32),
            jax.ShapeDtypeStruct((1, R), F32),
        ),
        in_specs=[any_spec, vm, any_spec, any_spec, any_spec, any_spec],
        out_specs=(vm, vm),
        scratch_shapes=[
            V((2, R, C), BF16),
            V((W, 1, C), F32),
            V((W, 2, C), BF16),
            V((S, 2, NTL), jnp.int32),
            V((1, 2 * coeffs), BF16),
            V((1, coeffs), F32),
            V((NT, C), F32),
            V((NT, C), F32),
            V((R, 2 * C), BF16),
            V((R, 2 * C), BF16),
            V((W, C), F32),
            V((W, C), F32),
            V((H, 2 * R), F32),
            V((max(S - 1, 1), H, 2 * R), F32),
            V((H, 2 * R), F32),
            V((R, C), F32),
            V((rows, 2 * R), F32),
            V((max(S - 1, 1), rows, 2 * R), F32),
            V((rows, 2 * R), F32),
            V((2, rows, R), BF16),
            V((H, 2 * R), F32),
            V((W, 2, C + G), F32),
            V((W // 2, 2, C + G), F32),
            V((W // 2, 2, C + G), F32),
            V((2, C + G), F32),
            V((S, 4, C), F32),
            dma((2,)), dma((4,)),
            dma((2, W // 2)), dma((2, W)), dma((2, W)),
            dma((S,)), dma((S,)),
            dma((S, NB + 1)), dma((S, NB + 1)),
            dma((W // 2,)), dma((W // 2,)),
            dma((W // 2,)), dma((W // 2,)),
            dma((S,)), dma((S,)),
        ],
        compiler_params=pltpu.CompilerParams(
            collective_id=0, has_side_effects=True, vmem_limit_bytes=60 * 1024 * 1024
        ),
    )(
        particles, group_id.reshape(1, R), ctf_curves, projections, inv_noise, shifts.T,
    )
    out, ev = pl.pallas_call(
        unfold,
        out_shape=(
            jax.ShapeDtypeStruct((1, 3 * coeffs), F32),
            jax.ShapeDtypeStruct((1, R), F32),
        ),
        in_specs=[vm, vm],
        out_specs=(vm, vm),
    )(out, ev)
    return out, ev.reshape(R)


def solution(mesh):
    W, S = mesh.shape["wide"], mesh.shape["shift"]
    placed = (
        P("wide", None),
        P("wide", None),
        P("wide", None),
        P("wide", None),
        P(),
        P("shift", None),
    )
    return jax.shard_map(
        functools.partial(local, W, S), mesh=mesh, in_specs=placed,
        out_specs=(P("wide", None), P("wide")), check_vma=False,
    )
```

profile of v0, /device:TPU:0, one launch (start us, length us, event | category | flops | bytes accessed | tf_op | source)
XLA Modules:
  0.0 37.7 jit_solution(15703677593985618559)
XLA Ops:
  0.6 35.5 %shard_map.77 = (f32[3,4224]{1,0:T(4,128)}, f32[1,64]{1,0:T(1,128)}) custom-call(bf16[64,8448]{1,0:T(8,128)(2,1)} %x_hbm.1, s32[1,64]{1,0:T(1,128)} %bitcast.4, f32[1,4224]{1,0:T(1,128)} %ctf_ref.1, bf16[1,8448]{1,0:T(2,128)(2,1)} %proj_ref.1, f32[4224]{0:T(1024)} %noise_ref.1, s32[2,32]{1,0:T(2,128)} %bitcast.3), custom_call_target="tpu_custom_call" | custom-call | tf_op jit(solution)/shard_map/pallas_call | solution.py:429
  36.2 1.5 %shard_map.78 = (f32[1,12672]{1,0:T(1,128)}, f32[1,64]{1,0:T(1,128)}) custom-call(f32[3,4224]{1,0:T(4,128)} %get-tuple-element.6.rows_ref, f32[1,64]{1,0:T(1,128)} %get-tuple-element.7.ev_in), custom_call_target="tpu_custom_call" | custom-call | tf_op jit(solution)/shard_map/pallas_call | solution.py:478
where the time goes:
time: 37.9 us; the launch traced here: 37.7 us
  Pallas kernels  37.1 us (98%)
  between operations  0.64 us (2%)
    pallas_call x1, Pallas kernels, local(): pl.pallas_call(functools.partial(kernel, (W, S, nl, L, NTL, R)), out_shap...  35.5 us
    pallas_call x1, Pallas kernels, local(): pl.pallas_call(unfold, out_shape=(jax.ShapeDtypeStruct((1, 3 * coeffs), F...  1.52 us

commit v1 on v0

v1 whole, which is shorter than its diff:
```python
import functools
import math

import jax
import jax.numpy as jnp
from jax import lax
from jax.experimental import pallas as pl
from jax.experimental.pallas import tpu as pltpu
from jax.sharding import PartitionSpec as P

LANE = 128
REACH = 8
NR = 2 * REACH + 1
PARTS = 3
STEP = 2.0 * math.pi / 128.0
HIGH = lax.Precision.HIGHEST
MESH = pl.DeviceIdType.MESH
F32 = jnp.float32
BF16 = jnp.bfloat16
NT_DIMS = (((1,), (1,)), ((), ()))
NN_DIMS = (((1,), (0,)), ((), ()))
TN_DIMS = (((0,), (0,)), ((), ()))


def dot(a, b, dims=NN_DIMS, precision=None):
    return lax.dot_general(a, b, dims, precision=precision, preferred_element_type=F32)


def turn(m):
    x = m - 128.0 * jnp.floor(m * (1.0 / 128.0) + 0.5)
    z = (32.0 - jnp.abs(x)) * STEP
    y = z * z
    p = 1.0 / 362880.0 - y * (1.0 / 39916800.0)
    p = -1.0 / 5040.0 + y * p
    p = 1.0 / 120.0 + y * p
    p = -1.0 / 6.0 + y * p
    return z + z * (y * p)


def cuts(L):
    n = min(PARTS, L)
    return [(L * c // n, L * (c + 1) // n) for c in range(n)]


def padded(n, m):
    return -(-n // m) * m


def kernel(
    cfg, x_hbm, gid_hbm, ctf_ref, proj_ref, noise_ref, sh_ref,
    out_ref, ev_ref,
    gid_ref, xbuf, cbuf, pbuf, shbuf, prow, nbuf, cos_t, sin_t, wgt, fil, evb, wsq, power, selfc, selfr, selft, rowbuf,
    sc, scr, tot, at, cs, w2, part, r1, stage, snd, r2, fbuf, obuf,
    x_sem, own_sem, ag_ssem, ag_rsem, mt_rsem, sh_ssem, sh_rsem,
    sc_ssem, sf_ssem, sc_rsem, r1_ssem, r1_rsem, r2_ssem, r2_rsem, f_ssem, f_rsem, o_sem,
):
    W, S, nl, L, NTL, R = cfg
    C = L * LANE
    NT = NTL * S
    H = W // 2
    NC = W // 2
    QB = 2
    NB = H // QB
    RB = QB * NT
    w = lax.axis_index("wide")
    s = lax.axis_index("shift")
    core = lax.rem(w, 2)
    chip = lax.div(w, 2)
    mate = chip * 2 + (1 - core)
    first = jnp.minimum(s * L, nl - L)
    start = pl.multiple_of(first * LANE, LANE)
    full = nl * LANE
    G = padded(W, LANE)
    window = pl.ds(start, C)

    def chip_at(k):
        return lax.rem(chip + k, NC)

    def remote(src, dst, ssem, rsem, wide=None, shift=None):
        return pltpu.make_async_remote_copy(
            src_ref=src, dst_ref=dst, send_sem=ssem, recv_sem=rsem,
            device_id=(w if wide is None else wide, s if shift is None else shift),
            device_id_type=MESH,
        )

    def settle(ref, sem):
        pltpu.make_async_copy(ref, ref, sem).wait()

    x_copies = [
        pltpu.make_async_copy(
            x_hbm.at[:, pl.ds(pl.multiple_of(start + h * full, LANE), C)],
            xbuf.at[h], x_sem,
        )
        for h in range(2)
    ]
    own = [
        pltpu.make_async_copy(ctf_ref.at[:, window], cbuf.at[w], own_sem.at[0]),
        pltpu.make_async_copy(proj_ref, prow, own_sem.at[1]),
        pltpu.make_async_copy(sh_ref, shbuf.at[s], own_sem.at[2]),
        pltpu.make_async_copy(noise_ref, nbuf.at[0], own_sem.at[3]),
        pltpu.make_async_copy(gid_hbm, gid_ref, own_sem.at[4]),
    ]
    for c in own + x_copies:
        c.start()

    bar = pltpu.get_barrier_semaphore()
    pl.semaphore_signal(bar, inc=1, device_id=(mate, s), device_id_type=MESH)

    def greet(k, carry):
        pl.semaphore_signal(
            bar, inc=1, device_id=(chip_at(k) * 2 + core, s), device_id_type=MESH
        )
        return carry

    lax.fori_loop(1, NC, greet, 0)
    for d in range(1, S):
        pl.semaphore_signal(
            bar, inc=1, device_id=(w, lax.rem(s + d, S)), device_id_type=MESH
        )
    own[1].wait()
    for h in range(2):
        pbuf[w, h : h + 1, :] = prow[:, pl.ds(pl.multiple_of(start + h * full, LANE), C)]

    pl.semaphore_wait(bar, NC + S - 1)

    def ag_pair(to, rsem):
        return (
            remote(ctf_ref.at[:, window], cbuf.at[w], ag_ssem.at[0], rsem, wide=to),
            remote(pbuf.at[w], pbuf.at[w], ag_ssem.at[1], rsem, wide=to),
        )

    def relay_pair(src):
        return (
            remote(cbuf.at[src], cbuf.at[src], ag_ssem.at[0], mt_rsem, wide=mate),
            remote(pbuf.at[src], pbuf.at[src], ag_ssem.at[1], mt_rsem, wide=mate),
        )

    sh_copies = [
        remote(sh_ref, shbuf.at[s], sh_ssem, sh_rsem, shift=lax.rem(s + d, S))
        for d in range(1, S)
    ]
    for c in sh_copies:
        c.start()

    def ag_start(k, carry):
        for c in ag_pair(chip_at(k) * 2 + core, ag_rsem.at[chip]):
            c.start()
        return carry

    lax.fori_loop(1, NC, ag_start, 0)
    for c in ag_pair(mate, mt_rsem):
        c.start()

    for c in own[:1] + own[2:]:
        c.wait()
    settle(shbuf.at[: S - 1], sh_rsem)

    lane = lax.broadcasted_iota(jnp.int32, (2, 2 * LANE), 1)
    axis = lax.broadcasted_iota(jnp.int32, (2, 2 * LANE), 0)
    freq = jnp.where(
        lane < LANE, jnp.where(axis == 0, first + lane, 0), jnp.where(axis == 1, lane - LANE - 64, 0)
    ).astype(F32)
    ang = STEP * jnp.concatenate(
        [dot(shbuf[t].astype(F32), freq, TN_DIMS, HIGH) for t in range(S)], axis=0
    )
    ang_a, ang_b = ang[:, :LANE], ang[:, LANE:]
    kx = first + lax.broadcasted_iota(jnp.int32, (NT, LANE), 1)
    live = jnp.where(kx >= s * L, 1.0, 0.0)
    cos_b, sin_b = jnp.cos(ang_b), jnp.sin(ang_b)
    cos_a, sin_a = jnp.cos(ang_a) * live, jnp.sin(ang_a) * live
    for l in range(L):
        ca, sa = cos_a[:, l : l + 1], sin_a[:, l : l + 1]
        cols = pl.ds(l * LANE, LANE)
        cos_t[:, cols] = ca * cos_b - sa * sin_b
        sin_t[:, cols] = sa * cos_b + ca * sin_b

    qn = at.shape[0]
    q = lax.broadcasted_iota(jnp.int32, (qn, 2 * NT), 0).astype(F32)
    lanes = lax.broadcasted_iota(jnp.int32, (qn, 2 * NT), 1)
    line = jnp.floor((q + 0.5) * (1.0 / NR))
    kind = q - line * NR
    sx, sy = (
        jnp.concatenate([shbuf[t][a : a + 1, :] for t in range(S)] * 2, axis=1).astype(F32)
        for a in range(2)
    )
    far = jnp.abs(sy)
    even = jnp.where(far == kind, 1.0, 0.0)
    odd = jnp.where(far == kind - REACH, jnp.where(sy > 0.0, 1.0, -1.0), 0.0)
    val = jnp.where(kind <= REACH, even, odd)
    kx_q = line + lax.convert_element_type(first, F32)
    val = val * turn(sx * kx_q - jnp.where(lanes < NT, 0.0, 32.0))
    val = jnp.where(kx_q >= lax.convert_element_type(s * L, F32), val, 0.0)
    ones = jnp.where(jnp.logical_and(q == L * NR, lanes < NT), 1.0, 0.0)
    val = jnp.where(q < L * NR, val, ones)
    val_hi = val.astype(BF16)
    at[:, : 2 * NT] = val_hi
    at[:, 2 * NT :] = (val - val_hi.astype(F32)).astype(BF16)
    row = lax.broadcasted_iota(jnp.int32, (2 * REACH, LANE), 0)
    ky = lax.broadcasted_iota(jnp.int32, (2 * REACH, LANE), 1) - 64
    far_row = jnp.where(row < REACH, row + 1, row + 1 - REACH)
    cs[...] = turn((far_row * ky).astype(F32) - jnp.where(row < REACH, 0.0, 32.0))

    def relay(k, carry):
        from_chip = lax.rem(chip + NC - k, NC)
        settle(cbuf.at[:2], ag_rsem.at[from_chip])
        for c in relay_pair(from_chip * 2 + core):
            c.start()
        return carry

    lax.fori_loop(1, NC, relay, 0)
    settle(cbuf.at[:W], mt_rsem)
    settle(xbuf, x_sem)

    onehot = jnp.where(
        gid_ref[...] == lax.broadcasted_iota(jnp.int32, (G, R), 0), 1.0, 0.0
    )
    pick = onehot[:W]
    for l in range(L):
        cols = pl.ds(l * LANE, LANE)
        curves = cbuf[:, 0, cols]
        row = dot(pick, curves, TN_DIMS, HIGH)
        noise = nbuf[:, pl.ds(pl.multiple_of(start + l * LANE, LANE), LANE)]
        x_re = xbuf[0, :, cols].astype(F32)
        x_im = xbuf[1, :, cols].astype(F32)
        gain = noise * row
        re, im = pl.ds(2 * l * LANE, LANE), pl.ds((2 * l + 1) * LANE, LANE)
        wgt[:, re] = (gain * x_re).astype(BF16)
        wgt[:, im] = (gain * x_im).astype(BF16)
        rowbuf[:, cols] = row

    def sc_copy(b, d):
        rows = pl.ds(pl.multiple_of(b * RB, RB), RB)
        return remote(
            sc.at[rows], scr.at[d - 1, rows], sc_ssem, sc_rsem.at[d - 1, b],
            shift=lax.rem(s + d, S),
        )

    def score_block(b, carry):
        acc = jnp.zeros((2 * RB, R), F32)
        for l in range(L):
            cols = pl.ds(l * LANE, LANE)
            ct, st = cos_t[:, cols], sin_t[:, cols]
            rots = []
            for h in range(2):
                for q in range(QB):
                    o = h * H + b * QB + q
                    pair = pbuf[o, :, cols].astype(F32)
                    pr, pi = pair[0:1], pair[1:2]
                    rots.append(
                        jnp.concatenate(
                            [(pr * ct + pi * st).astype(BF16), (pi * ct - pr * st).astype(BF16)],
                            axis=1,
                        )
                    )
            rot = jnp.concatenate(rots, axis=0)
            acc = acc + dot(rot, wgt[:, pl.ds(2 * l * LANE, 2 * LANE)], NT_DIMS)
        both = jnp.concatenate([acc[:RB], acc[RB:]], axis=1)
        sc[pl.ds(pl.multiple_of(b * RB, RB), RB), :] = both
        for d in range(1, S):
            sc_copy(b, d).start()
        return carry

    lax.fori_loop(0, NB, score_block, 0)

    def square(o, carry):
        p = pbuf[o].astype(F32)
        power[pl.ds(o, 1), :] = jnp.sum(p * p, axis=0, keepdims=True)
        return carry

    lax.fori_loop(0, W, square, 0)
    for l in range(L):
        cols = pl.ds(l * LANE, LANE)
        curves = cbuf[:, 0, cols]
        noise = nbuf[:, pl.ds(pl.multiple_of(start + l * LANE, LANE), LANE)]
        here = jnp.where(first + l >= s * L, 0.5, 0.0)
        wsq[:, cols] = curves * curves * noise * here
    self_g = dot(power[...], wsq[...], NT_DIMS, HIGH)
    self_i = dot(self_g, pick, NN_DIMS, HIGH)
    selfc[...] = jnp.concatenate([self_i[:H], self_i[H:]], axis=1)

    def self_copy(d):
        return remote(
            selfc, selfr.at[d - 1], sf_ssem, sc_rsem.at[d - 1, NB],
            shift=lax.rem(s + d, S),
        )

    for d in range(1, S):
        self_copy(d).start()
    for l in range(L):
        cols = pl.ds(l * LANE, LANE)
        row = rowbuf[:, cols]
        f_re = row * xbuf[0, :, cols].astype(F32)
        f_im = row * xbuf[1, :, cols].astype(F32)
        re, im = pl.ds(2 * l * LANE, LANE), pl.ds((2 * l + 1) * LANE, LANE)
        fil[:, re] = jnp.concatenate([f_re, -f_im], axis=0).astype(BF16)
        fil[:, im] = jnp.concatenate([f_im, f_re], axis=0).astype(BF16)
    self_all = selfc[...]
    for d in range(1, S):
        self_copy(d).wait_recv()
        self_all = self_all + selfr[d - 1]
    selft[...] = self_all

    def swap(v):
        return pltpu.roll(v, R, 1)

    def join(b, m):
        rows = pl.ds(pl.multiple_of(b * RB, RB), RB)
        v = sc[rows, :]
        for d in range(1, S):
            sc_copy(b, d).wait_recv()
            v = v + scr[d - 1, rows, :]
        for q in range(QB):
            u = v[q * NT : (q + 1) * NT] - selft[pl.ds(b * QB + q, 1), :]
            tot[pl.ds(pl.multiple_of(b * RB + q * NT, NT), NT), :] = u
            m = jnp.maximum(m, jnp.max(u.reshape(NT // 8, 8, 2 * R), axis=0))
        return m

    m8 = lax.fori_loop(0, NB, join, jnp.full((8, 2 * R), -jnp.inf, F32))
    top = jnp.max(m8, axis=0, keepdims=True)
    top = jnp.maximum(top, swap(top))

    def expo(b, t):
        rows = pl.ds(pl.multiple_of(b * RB, RB), RB)
        e = jnp.exp(tot[rows, :] - top)
        tot[rows, :] = e
        return t + jnp.sum(e.reshape(RB // 8, 8, 2 * R), axis=0)

    t8 = lax.fori_loop(0, NB, expo, jnp.zeros((8, 2 * R), F32))
    total = jnp.sum(t8, axis=0, keepdims=True)
    total = total + swap(total)
    evb[...] = (top + jnp.log(total))[:, :R]
    ev_copy = pltpu.make_async_copy(evb, ev_ref, o_sem.at[0])
    ev_copy.start()

    half = lax.broadcasted_iota(jnp.int32, (NT, 2 * R), 1) < R
    for o in range(H):
        v = tot[o * NT : (o + 1) * NT, :] / total
        a, b = jnp.where(half, v, 0.0), jnp.where(half, 0.0, v)
        cols = []
        for lo, hi in ((a, swap(a)), (swap(b), b)):
            two = jnp.concatenate([lo, hi], axis=0).astype(BF16)
            cols.append(jnp.concatenate([two, two], axis=0))
        out = dot(at[...], jnp.concatenate(cols, axis=1))
        for h in range(2):
            n = h * H + o
            w2[pl.ds((n % 2) * H + n // 2, qn, stride=W), :] = out[:, h * 2 * R : (h + 1) * 2 * R]

    pieces = cuts(L)
    NP = len(pieces)

    def span(c):
        lo, hi = pieces[c]
        return 2 * lo * LANE, 2 * hi * LANE + (G if c == NP - 1 else 0)

    def r1_copy(c):
        lo, hi = span(c)
        rows = pl.ds(pl.multiple_of((1 - core) * H, 8), H)
        return remote(
            part.at[rows, lo:hi], r1.at[:, lo:hi], r1_ssem, r1_rsem.at[c], wide=mate
        )

    RP = stage.shape[0] // NC // NP

    def r2_copy(k, c):
        to = chip_at(k)
        rows = pl.ds(pl.multiple_of(c * RP, 8), RP)
        return remote(
            snd.at[to, rows], r2.at[k, rows], r2_ssem, r2_rsem.at[c],
            wide=2 * to + core,
        )

    mine = pl.ds(pl.multiple_of(core * H, 8), H)
    waves = cs[...]

    def update(c):
        lo, hi = pieces[c]
        for l in range(lo, hi):
            lhs = w2[l * NR * W : (l + 1) * NR * W, :].astype(BF16)
            u = dot(lhs, fil[:, 2 * l * LANE : (2 * l + 2) * LANE])
            u_re, u_im = u[:, :LANE], u[:, LANE:]
            re, im = u_re[:W], u_im[:W]
            for r in range(REACH):
                e = slice((r + 1) * W, (r + 2) * W)
                d = slice((r + 1 + REACH) * W, (r + 2 + REACH) * W)
                c_r, s_r = waves[r : r + 1], waves[REACH + r : REACH + r + 1]
                re = re + (u_re[e] * c_r - u_im[d] * s_r)
                im = im + (u_im[e] * c_r + u_re[d] * s_r)
            part[:, 2 * l * LANE : (2 * l + 1) * LANE] = re
            part[:, (2 * l + 1) * LANE : (2 * l + 2) * LANE] = im
        if c == NP - 1:
            load = w2[L * NR * W : L * NR * W + W, :R]
            part[:, 2 * C : 2 * C + G] = dot(load, onehot, NT_DIMS, HIGH)

    def put(c, i, v):
        stage[pl.ds(c * NC * RP + i, NC, stride=RP), :] = v

    def pass_on(c):
        r1_copy(c).wait_recv()
        lo, hi = pieces[c]
        for i in range(2 * (hi - lo)):
            cols = pl.ds((2 * lo + i) * LANE, LANE)
            put(c, i, part[mine, cols] + r1[:, cols])
        if c == NP - 1:
            for g in range(G // LANE):
                cols = pl.ds(2 * C + g * LANE, LANE)
                rest = part[mine, cols] + r1[:, cols]
                for p in range(3):
                    top_part = rest.astype(BF16).astype(F32)
                    put(c, 2 * (hi - lo) + 3 * g + p, top_part)
                    rest = rest - top_part
        for j in range(NC):
            at_row = (c * NC + j) * RP
            snd[j, c * RP : (c + 1) * RP, :] = stage[at_row : at_row + RP, :].astype(BF16)

        def go(k, carry):
            r2_copy(k, c).start()
            return carry

        lax.fori_loop(1, NC, go, 0)

    for c in range(NP):
        update(c)
        r1_copy(c).start()
        if c:
            pass_on(c - 1)
    pass_on(NP - 1)
    curves = cbuf[:, 0, :]
    squares = curves * curves
    for c in range(NP):
        def take(k, acc):
            return acc + r2[k, c * RP : (c + 1) * RP, :].astype(F32)

        settle(r2.at[1:, c * RP : (c + 1) * RP], r2_rsem.at[c])
        own_rows = stage[pl.ds(pl.multiple_of((c * NC + chip) * RP, 8), RP), :]
        acc = lax.fori_loop(1, NC, take, own_rows)
        lo, hi = pieces[c]
        for l in range(lo, hi):
            i = 2 * (l - lo)
            fbuf[s, l : l + 1, :] = acc[i : i + 1]
            fbuf[s, L + l : L + l + 1, :] = acc[i + 1 : i + 2]
    base = 2 * (pieces[-1][1] - pieces[-1][0])
    load = jnp.concatenate(
        [
            acc[base + 3 * g : base + 3 * g + 1]
            + acc[base + 3 * g + 1 : base + 3 * g + 2]
            + acc[base + 3 * g + 2 : base + 3 * g + 3]
            for g in range(G // LANE)
        ],
        axis=1,
    )[:, :W]
    spread = dot(load, squares, precision=HIGH)
    for l in range(L):
        fbuf[s, 2 * L + l : 2 * L + l + 1, :] = spread[:, l * LANE : (l + 1) * LANE]

    def f_copy(d):
        return remote(
            fbuf.at[s], fbuf.at[s], f_ssem, f_rsem, shift=lax.rem(s + d, S)
        )

    for d in range(1, S):
        f_copy(d).start()
    settle(fbuf.at[: S - 1], f_rsem)
    for t in range(S):
        lo, hi = t * L, min(t * L + L, nl)
        if lo < hi:
            off = lo - min(lo, nl - L)
            for r in range(3):
                obuf[r * nl + lo : r * nl + hi, :] = fbuf[t, r * L + off : r * L + off + hi - lo, :]
    out_copy = pltpu.make_async_copy(obuf, out_ref, o_sem.at[1])
    out_copy.start()

    settle(shbuf.at[: S - 1], sh_ssem)
    settle(cbuf.at[: W - 1], ag_ssem.at[0])
    settle(pbuf.at[: W - 1], ag_ssem.at[1])
    settle(r1, r1_ssem)
    settle(snd.at[: NC - 1], r2_ssem)
    settle(scr.at[: S - 1], sc_ssem)
    settle(selfr.at[: S - 1], sf_ssem)
    settle(fbuf.at[: S - 1], f_ssem)
    ev_copy.wait()
    out_copy.wait()


def unfold(rows_ref, ev_in, out_ref, ev_ref):
    for r in range(rows_ref.shape[0]):
        out_ref[:, r * LANE : (r + 1) * LANE] = rows_ref[r : r + 1, :]
    ev_ref[...] = ev_in[...]


def local(W, S, particles, group_id, ctf_curves, projections, inv_noise, shifts):
    R = particles.shape[0]
    coeffs = inv_noise.shape[0]
    nl = coeffs // LANE
    L = -(-nl // S)
    C = L * LANE
    NTL = shifts.shape[0]
    NT = NTL * S
    H = W // 2
    NB = H // 2
    G = padded(W, LANE)
    rows = H * NT
    qn = padded(L * NR + 1, 16)
    pieces = cuts(L)
    RP = padded(max(2 * (hi - lo) for lo, hi in pieces) + 3 * G // LANE, 16)
    NP = len(pieces)
    any_spec = pl.BlockSpec(memory_space=pl.ANY)
    vm = pl.BlockSpec(memory_space=pltpu.VMEM)
    dma = pltpu.SemaphoreType.DMA
    V = pltpu.VMEM
    out, ev = pl.pallas_call(
        functools.partial(kernel, (W, S, nl, L, NTL, R)),
        out_shape=(
            jax.ShapeDtypeStruct((3 * nl, LANE), F32),
            jax.ShapeDtypeStruct((1, R), F32),
        ),
        in_specs=[any_spec] * 6,
        out_specs=(any_spec, any_spec),
        scratch_shapes=[
            V((1, R), jnp.int32),
            V((2, R, C), BF16),
            V((W, 1, C), F32),
            V((W, 2, C), BF16),
            V((S, 2, NTL), jnp.int32),
            V((1, 2 * coeffs), BF16),
            V((1, coeffs), F32),
            V((NT, C), F32),
            V((NT, C), F32),
            V((R, 2 * C), BF16),
            V((2 * R, 2 * C), BF16),
            V((1, R), F32),
            V((W, C), F32),
            V((W, C), F32),
            V((H, 2 * R), F32),
            V((max(S - 1, 1), H, 2 * R), F32),
            V((H, 2 * R), F32),
            V((R, C), F32),
            V((rows, 2 * R), F32),
            V((max(S - 1, 1), rows, 2 * R), F32),
            V((rows, 2 * R), F32),
            V((qn, 4 * NT), BF16),
            V((2 * REACH, LANE), F32),
            V((qn * W, 2 * R), F32),
            V((W, 2 * C + G), F32),
            V((H, 2 * C + G), F32),
            V((H * NP * RP, LANE), F32),
            V((H, NP * RP, LANE), BF16),
            V((H, NP * RP, LANE), BF16),
            V((S, padded(3 * L, 8), LANE), F32),
            V((3 * nl, LANE), F32),
            dma(()), dma((5,)),
            dma((2,)), dma((W // 2,)), dma(()), dma(()), dma(()),
            dma(()), dma(()), dma((max(S - 1, 1), NB + 1)),
            dma(()), dma((NP,)), dma(()), dma((NP,)),
            dma(()), dma(()), dma((2,)),
        ],
        compiler_params=pltpu.CompilerParams(
            collective_id=0, has_side_effects=True, vmem_limit_bytes=60 * 1024 * 1024
        ),
    )(
        particles, group_id.reshape(1, R), ctf_curves, projections, inv_noise, shifts.T,
    )
    out, ev = pl.pallas_call(
        unfold,
        out_shape=(
            jax.ShapeDtypeStruct((1, 3 * coeffs), F32),
            jax.ShapeDtypeStruct((1, R), F32),
        ),
        in_specs=[vm, vm],
        out_specs=(vm, vm),
    )(out, ev)
    return out, ev.reshape(R)


def solution(mesh):
    W, S = mesh.shape["wide"], mesh.shape["shift"]
    placed = (
        P("wide", None),
        P("wide", None),
        P("wide", None),
        P("wide", None),
        P(),
        P("shift", None),
    )
    return jax.shard_map(
        functools.partial(local, W, S), mesh=mesh, in_specs=placed,
        out_specs=(P("wide", None), P("wide")), check_vma=False,
    )
```

time: 37.9 us -> 35.5 us (0.937)
  Pallas kernels: 37.1 us -> 34.7 us
    pallas_call x1, Pallas kernels: 35.5 us -> 33.2 us  [local(): pl.pallas_call(functools.partial(kernel, (W, S, nl, L, NTL, R)), out_shap...]
where the time goes in v1:
time: 35.5 us; the launch traced here: 35.3 us
  Pallas kernels  34.7 us (98%)
  between operations  0.64 us (2%)
    pallas_call x1, Pallas kernels, local(): pl.pallas_call(functools.partial(kernel, (W, S, nl, L, NTL, R)), out_shap...  33.2 us
    pallas_call x1, Pallas kernels, local(): pl.pallas_call(unfold, out_shape=(jax.ShapeDtypeStruct((1, 3 * coeffs), F...  1.47 us

profile of v1, /device:TPU:0, one launch (start us, length us, event | category | flops | bytes accessed | tf_op | source)
XLA Modules:
  0.0 35.3 jit_solution(3459092545726412829)
XLA Ops:
  0.6 33.2 %shard_map.77 = (f32[99,128]{1,0:T(8,128)}, f32[1,64]{1,0:T(1,128)}) custom-call(bf16[64,8448]{1,0:T(8,128)(2,1)} %x_hbm.1, s32[1,64]{1,0:T(1,128)} %bitcast.4, f32[1,4224]{1,0:T(1,128)} %ctf_ref.1, bf16[1,8448]{1,0:T(2,128)(2,1)} %proj_ref.1, f32[4224]{0:T(1024)} %noise_ref.1, s32[2,32]{1,0:T(2,128)} %bitcast.3), custom_call_target="tpu_custom_call" | custom-call | tf_op jit(solution)/shard_map/pallas_call | solution.py:510
  33.8 1.5 %shard_map.78 = (f32[1,12672]{1,0:T(1,128)}, f32[1,64]{1,0:T(1,128)}) custom-call(f32[99,128]{1,0:T(8,128)} %get-tuple-element.6.rows_ref, f32[1,64]{1,0:T(1,128)} %get-tuple-element.7.ev_in), custom_call_target="tpu_custom_call" | custom-call | tf_op jit(solution)/shard_map/pallas_call | solution.py:562

commit v2 on v1

--- a/solution.py
+++ b/solution.py
@@ -10,6 +10,7 @@
 
 LANE = 128
 REACH = 8
+FULL = 32767.0
 NR = 2 * REACH + 1
 PARTS = 3
 STEP = 2.0 * math.pi / 128.0
@@ -200,12 +201,19 @@
     far_row = jnp.where(row < REACH, row + 1, row + 1 - REACH)
     cs[...] = turn((far_row * ky).astype(F32) - jnp.where(row < REACH, 0.0, 32.0))
 
+    def square(o, carry):
+        p = pbuf[o].astype(F32)
+        power[pl.ds(o, 1), :] = jnp.sum(p * p, axis=0, keepdims=True)
+        return carry
+
+    square(w, 0)
+
     def relay(k, carry):
         from_chip = lax.rem(chip + NC - k, NC)
         settle(cbuf.at[:2], ag_rsem.at[from_chip])
         for c in relay_pair(from_chip * 2 + core):
             c.start()
-        return carry
+        return square(from_chip * 2 + core, carry)
 
     lax.fori_loop(1, NC, relay, 0)
     settle(cbuf.at[:W], mt_rsem)
@@ -255,19 +263,21 @@
             rot = jnp.concatenate(rots, axis=0)
             acc = acc + dot(rot, wgt[:, pl.ds(2 * l * LANE, 2 * LANE)], NT_DIMS)
         both = jnp.concatenate([acc[:RB], acc[RB:]], axis=1)
-        sc[pl.ds(pl.multiple_of(b * RB, RB), RB), :] = both
+        peak = jnp.max(jnp.abs(both).reshape(RB // 8, 8, 2 * R), axis=0)
+        peak = jnp.maximum(jnp.max(peak, axis=0, keepdims=True), 1e-30)
+        code = jnp.floor(both * (FULL / peak) + 0.5).astype(jnp.int32).astype(jnp.int16)
+        sc[pl.ds(pl.multiple_of(b * RB, RB), RB), :] = code
+        selfc[pl.ds(H + b, 1), :] = peak * (1.0 / FULL)
         for d in range(1, S):
             sc_copy(b, d).start()
         return carry
 
     lax.fori_loop(0, NB, score_block, 0)
 
-    def square(o, carry):
-        p = pbuf[o].astype(F32)
-        power[pl.ds(o, 1), :] = jnp.sum(p * p, axis=0, keepdims=True)
-        return carry
-
-    lax.fori_loop(0, W, square, 0)
+    def square_mate(j, carry):
+        return square(j * 2 + (1 - core), carry)
+
+    lax.fori_loop(0, NC, square_mate, 0)
     for l in range(L):
         cols = pl.ds(l * LANE, LANE)
         curves = cbuf[:, 0, cols]
@@ -276,7 +286,7 @@
         wsq[:, cols] = curves * curves * noise * here
     self_g = dot(power[...], wsq[...], NT_DIMS, HIGH)
     self_i = dot(self_g, pick, NN_DIMS, HIGH)
-    selfc[...] = jnp.concatenate([self_i[:H], self_i[H:]], axis=1)
+    selfc[:H, :] = jnp.concatenate([self_i[:H], self_i[H:]], axis=1)
 
     def self_copy(d):
         return remote(
@@ -294,10 +304,10 @@
         re, im = pl.ds(2 * l * LANE, LANE), pl.ds((2 * l + 1) * LANE, LANE)
         fil[:, re] = jnp.concatenate([f_re, -f_im], axis=0).astype(BF16)
         fil[:, im] = jnp.concatenate([f_im, f_re], axis=0).astype(BF16)
-    self_all = selfc[...]
+    self_all = selfc[:H, :]
     for d in range(1, S):
         self_copy(d).wait_recv()
-        self_all = self_all + selfr[d - 1]
+        self_all = self_all + selfr[d - 1, :H, :]
     selft[...] = self_all
 
     def swap(v):
@@ -305,10 +315,11 @@
 
     def join(b, m):
         rows = pl.ds(pl.multiple_of(b * RB, RB), RB)
-        v = sc[rows, :]
+        v = sc[rows, :].astype(jnp.int32).astype(F32) * selfc[pl.ds(H + b, 1), :]
         for d in range(1, S):
             sc_copy(b, d).wait_recv()
-            v = v + scr[d - 1, rows, :]
+            other = scr[d - 1, rows, :].astype(jnp.int32).astype(F32)
+            v = v + other * selfr[d - 1, pl.ds(H + b, 1), :]
         for q in range(QB):
             u = v[q * NT : (q + 1) * NT] - selft[pl.ds(b * QB + q, 1), :]
             tot[pl.ds(pl.multiple_of(b * RB + q * NT, NT), NT), :] = u
@@ -530,12 +541,12 @@
             V((1, R), F32),
             V((W, C), F32),
             V((W, C), F32),
-            V((H, 2 * R), F32),
-            V((max(S - 1, 1), H, 2 * R), F32),
+            V((H + NB, 2 * R), F32),
+            V((max(S - 1, 1), H + NB, 2 * R), F32),
             V((H, 2 * R), F32),
             V((R, C), F32),
-            V((rows, 2 * R), F32),
-            V((max(S - 1, 1), rows, 2 * R), F32),
+            V((rows, 2 * R), jnp.int16),
+            V((max(S - 1, 1), rows, 2 * R), jnp.int16),
             V((rows, 2 * R), F32),
             V((qn, 4 * NT), BF16),
             V((2 * REACH, LANE), F32),

time: 35.5 us -> 34.1 us (0.961)
  Pallas kernels: 34.7 us -> 33.3 us
    pallas_call x1, Pallas kernels: 33.2 us -> 31.8 us  [local(): pl.pallas_call(functools.partial(kernel, (W, S, nl, L, NTL, R)), out_shap...]
where the time goes in v2:
time: 34.1 us; the launch traced here: 33.9 us
  Pallas kernels  33.3 us (98%)
  between operations  0.64 us (2%)
    pallas_call x1, Pallas kernels, local(): pl.pallas_call(functools.partial(kernel, (W, S, nl, L, NTL, R)), out_shap...  31.8 us
    pallas_call x1, Pallas kernels, local(): pl.pallas_call(unfold, out_shape=(jax.ShapeDtypeStruct((1, 3 * coeffs), F...  1.47 us

profile of v2, /device:TPU:0, one launch (start us, length us, event | category | flops | bytes accessed | tf_op | source)
XLA Modules:
  0.0 33.9 jit_solution(10802140739194618802)
XLA Ops:
  0.6 31.8 %shard_map.77 = (f32[99,128]{1,0:T(8,128)}, f32[1,64]{1,0:T(1,128)}) custom-call(bf16[64,8448]{1,0:T(8,128)(2,1)} %x_hbm.1, s32[1,64]{1,0:T(1,128)} %bitcast.4, f32[1,4224]{1,0:T(1,128)} %ctf_ref.1, bf16[1,8448]{1,0:T(2,128)(2,1)} %proj_ref.1, f32[4224]{0:T(1024)} %noise_ref.1, s32[2,32]{1,0:T(2,128)} %bitcast.3), custom_call_target="tpu_custom_call" | custom-call | tf_op jit(solution)/shard_map/pallas_call | solution.py:521
  32.4 1.5 %shard_map.78 = (f32[1,12672]{1,0:T(1,128)}, f32[1,64]{1,0:T(1,128)}) custom-call(f32[99,128]{1,0:T(8,128)} %get-tuple-element.6.rows_ref, f32[1,64]{1,0:T(1,128)} %get-tuple-element.7.ev_in), custom_call_target="tpu_custom_call" | custom-call | tf_op jit(solution)/shard_map/pallas_call | solution.py:573

commit v3 on v2

--- a/solution.py
+++ b/solution.py
@@ -38,6 +38,13 @@
     return z + z * (y * p)
 
 
+def split3(v):
+    hi = v.astype(BF16)
+    rest = v - hi.astype(F32)
+    mid = rest.astype(BF16)
+    return [hi, mid, (rest - mid.astype(F32)).astype(BF16)]
+
+
 def cuts(L):
     n = min(PARTS, L)
     return [(L * c // n, L * (c + 1) // n) for c in range(n)]
@@ -51,7 +58,7 @@
     cfg, x_hbm, gid_hbm, ctf_ref, proj_ref, noise_ref, sh_ref,
     out_ref, ev_ref,
     gid_ref, xbuf, cbuf, pbuf, shbuf, prow, nbuf, cos_t, sin_t, wgt, fil, evb, wsq, power, selfc, selfr, selft, rowbuf,
-    sc, scr, tot, at, cs, w2, part, r1, stage, snd, r2, fbuf, obuf,
+    sc, scr, tot, at, cs, w2, part, r1, stage, snd, r2, fdat, fwt,
     x_sem, own_sem, ag_ssem, ag_rsem, mt_rsem, sh_ssem, sh_rsem,
     sc_ssem, sf_ssem, sc_rsem, r1_ssem, r1_rsem, r2_ssem, r2_rsem, f_ssem, f_rsem, o_sem,
 ):
@@ -223,10 +230,11 @@
         gid_ref[...] == lax.broadcasted_iota(jnp.int32, (G, R), 0), 1.0, 0.0
     )
     pick = onehot[:W]
+    pick3 = jnp.concatenate([pick] * 3, axis=0).astype(BF16)
     for l in range(L):
         cols = pl.ds(l * LANE, LANE)
         curves = cbuf[:, 0, cols]
-        row = dot(pick, curves, TN_DIMS, HIGH)
+        row = dot(pick3, jnp.concatenate(split3(curves), axis=0), TN_DIMS)
         noise = nbuf[:, pl.ds(pl.multiple_of(start + l * LANE, LANE), LANE)]
         x_re = xbuf[0, :, cols].astype(F32)
         x_im = xbuf[1, :, cols].astype(F32)
@@ -284,8 +292,11 @@
         noise = nbuf[:, pl.ds(pl.multiple_of(start + l * LANE, LANE), LANE)]
         here = jnp.where(first + l >= s * L, 0.5, 0.0)
         wsq[:, cols] = curves * curves * noise * here
-    self_g = dot(power[...], wsq[...], NT_DIMS, HIGH)
-    self_i = dot(self_g, pick, NN_DIMS, HIGH)
+    p3, q3 = split3(power[...]), split3(wsq[...])
+    left = jnp.concatenate([p3[0], p3[0], p3[1], p3[1], p3[0], p3[2]], axis=1)
+    right = jnp.concatenate([q3[0], q3[1], q3[0], q3[1], q3[2], q3[0]], axis=1)
+    self_g = dot(left, right, NT_DIMS)
+    self_i = dot(jnp.concatenate(split3(self_g), axis=1), pick3)
     selfc[:H, :] = jnp.concatenate([self_i[:H], self_i[H:]], axis=1)
 
     def self_copy(d):
@@ -361,7 +372,7 @@
 
     def span(c):
         lo, hi = pieces[c]
-        return 2 * lo * LANE, 2 * hi * LANE + (G if c == NP - 1 else 0)
+        return 2 * lo * LANE + (G if c else 0), 2 * hi * LANE + G
 
     def r1_copy(c):
         lo, hi = span(c)
@@ -385,6 +396,9 @@
 
     def update(c):
         lo, hi = pieces[c]
+        if c == 0:
+            load = w2[L * NR * W : L * NR * W + W, :R]
+            part[:, :G] = dot(load, onehot, NT_DIMS, HIGH)
         for l in range(lo, hi):
             lhs = w2[l * NR * W : (l + 1) * NR * W, :].astype(BF16)
             u = dot(lhs, fil[:, 2 * l * LANE : (2 * l + 2) * LANE])
@@ -396,12 +410,9 @@
                 c_r, s_r = waves[r : r + 1], waves[REACH + r : REACH + r + 1]
                 re = re + (u_re[e] * c_r - u_im[d] * s_r)
                 im = im + (u_im[e] * c_r + u_re[d] * s_r)
-            part[:, 2 * l * LANE : (2 * l + 1) * LANE] = re
-            part[:, (2 * l + 1) * LANE : (2 * l + 2) * LANE] = im
-        if c == NP - 1:
-            load = w2[L * NR * W : L * NR * W + W, :R]
-            part[:, 2 * C : 2 * C + G] = dot(load, onehot, NT_DIMS, HIGH)
-
+            col = G + 2 * l * LANE
+            part[:, col : col + LANE] = re
+            part[:, col + LANE : col + 2 * LANE] = im
     def put(c, i, v):
         stage[pl.ds(c * NC * RP + i, NC, stride=RP), :] = v
 
@@ -409,11 +420,11 @@
         r1_copy(c).wait_recv()
         lo, hi = pieces[c]
         for i in range(2 * (hi - lo)):
-            cols = pl.ds((2 * lo + i) * LANE, LANE)
+            cols = pl.ds(G + (2 * lo + i) * LANE, LANE)
             put(c, i, part[mine, cols] + r1[:, cols])
-        if c == NP - 1:
+        if c == 0:
             for g in range(G // LANE):
-                cols = pl.ds(2 * C + g * LANE, LANE)
+                cols = pl.ds(g * LANE, LANE)
                 rest = part[mine, cols] + r1[:, cols]
                 for p in range(3):
                     top_part = rest.astype(BF16).astype(F32)
@@ -437,6 +448,13 @@
     pass_on(NP - 1)
     curves = cbuf[:, 0, :]
     squares = curves * curves
+
+    def deliver(src, row):
+        dst = out_ref.at[s, row : row + src.shape[0]]
+        for d in range(1, S):
+            remote(src, dst, f_ssem, f_rsem, shift=lax.rem(s + d, S)).start()
+        pltpu.make_async_copy(src, dst, o_sem.at[1]).start()
+
     for c in range(NP):
         def take(k, acc):
             return acc + r2[k, c * RP : (c + 1) * RP, :].astype(F32)
@@ -444,42 +462,26 @@
         settle(r2.at[1:, c * RP : (c + 1) * RP], r2_rsem.at[c])
         own_rows = stage[pl.ds(pl.multiple_of((c * NC + chip) * RP, 8), RP), :]
         acc = lax.fori_loop(1, NC, take, own_rows)
-        lo, hi = pieces[c]
-        for l in range(lo, hi):
-            i = 2 * (l - lo)
-            fbuf[s, l : l + 1, :] = acc[i : i + 1]
-            fbuf[s, L + l : L + l + 1, :] = acc[i + 1 : i + 2]
-    base = 2 * (pieces[-1][1] - pieces[-1][0])
-    load = jnp.concatenate(
-        [
-            acc[base + 3 * g : base + 3 * g + 1]
-            + acc[base + 3 * g + 1 : base + 3 * g + 2]
-            + acc[base + 3 * g + 2 : base + 3 * g + 3]
-            for g in range(G // LANE)
-        ],
-        axis=1,
-    )[:, :W]
-    spread = dot(load, squares, precision=HIGH)
-    for l in range(L):
-        fbuf[s, 2 * L + l : 2 * L + l + 1, :] = spread[:, l * LANE : (l + 1) * LANE]
-
-    def f_copy(d):
-        return remote(
-            fbuf.at[s], fbuf.at[s], f_ssem, f_rsem, shift=lax.rem(s + d, S)
-        )
-
-    for d in range(1, S):
-        f_copy(d).start()
-    settle(fbuf.at[: S - 1], f_rsem)
-    for t in range(S):
-        lo, hi = t * L, min(t * L + L, nl)
-        if lo < hi:
-            off = lo - min(lo, nl - L)
-            for r in range(3):
-                obuf[r * nl + lo : r * nl + hi, :] = fbuf[t, r * L + off : r * L + off + hi - lo, :]
-    out_copy = pltpu.make_async_copy(obuf, out_ref, o_sem.at[1])
-    out_copy.start()
-
+        fdat[c] = acc
+        deliver(fdat.at[c], c * RP)
+        if c == 0:
+            lo, hi = pieces[c]
+            base = 2 * (hi - lo)
+            load = jnp.concatenate(
+                [
+                    acc[base + 3 * g : base + 3 * g + 1]
+                    + acc[base + 3 * g + 1 : base + 3 * g + 2]
+                    + acc[base + 3 * g + 2 : base + 3 * g + 3]
+                    for g in range(G // LANE)
+                ],
+                axis=1,
+            )[:, :W]
+            spread = dot(load, squares, precision=HIGH)
+            for l in range(L):
+                fwt[l : l + 1, :] = spread[:, l * LANE : (l + 1) * LANE]
+            deliver(fwt, NP * RP)
+
+    settle(out_ref.at[: S - 1], f_rsem)
     settle(shbuf.at[: S - 1], sh_ssem)
     settle(cbuf.at[: W - 1], ag_ssem.at[0])
     settle(pbuf.at[: W - 1], ag_ssem.at[1])
@@ -487,14 +489,25 @@
     settle(snd.at[: NC - 1], r2_ssem)
     settle(scr.at[: S - 1], sc_ssem)
     settle(selfr.at[: S - 1], sf_ssem)
-    settle(fbuf.at[: S - 1], f_ssem)
+    settle(out_ref.at[: S - 1], f_ssem)
     ev_copy.wait()
-    out_copy.wait()
-
-
-def unfold(rows_ref, ev_in, out_ref, ev_ref):
-    for r in range(rows_ref.shape[0]):
-        out_ref[:, r * LANE : (r + 1) * LANE] = rows_ref[r : r + 1, :]
+    settle(out_ref.at[:1], o_sem.at[1])
+
+
+def unfold(nl, L, RP, rows_ref, ev_in, out_ref, ev_ref):
+    S = rows_ref.shape[0]
+    pieces = cuts(L)
+    for t in range(S):
+        first = min(t * L, nl - L)
+        for c, (lo, hi) in enumerate(pieces):
+            for l in range(lo, hi):
+                n = first + l
+                if n < t * L:
+                    continue
+                at_row = c * RP + 2 * (l - lo)
+                for r, row in enumerate((at_row, at_row + 1, len(pieces) * RP + l)):
+                    col = (r * nl + n) * LANE
+                    out_ref[:, col : col + LANE] = rows_ref[t, row : row + 1, :]
     ev_ref[...] = ev_in[...]
 
 
@@ -521,7 +534,7 @@
     out, ev = pl.pallas_call(
         functools.partial(kernel, (W, S, nl, L, NTL, R)),
         out_shape=(
-            jax.ShapeDtypeStruct((3 * nl, LANE), F32),
+            jax.ShapeDtypeStruct((S, NP * RP + padded(L, 8), LANE), F32),
             jax.ShapeDtypeStruct((1, R), F32),
         ),
         in_specs=[any_spec] * 6,
@@ -556,8 +569,8 @@
             V((H * NP * RP, LANE), F32),
             V((H, NP * RP, LANE), BF16),
             V((H, NP * RP, LANE), BF16),
-            V((S, padded(3 * L, 8), LANE), F32),
-            V((3 * nl, LANE), F32),
+            V((NP, RP, LANE), F32),
+            V((padded(L, 8), LANE), F32),
             dma(()), dma((5,)),
             dma((2,)), dma((W // 2,)), dma(()), dma(()), dma(()),
             dma(()), dma(()), dma((max(S - 1, 1), NB + 1)),
@@ -571,7 +584,7 @@
         particles, group_id.reshape(1, R), ctf_curves, projections, inv_noise, shifts.T,
     )
     out, ev = pl.pallas_call(
-        unfold,
+        functools.partial(unfold, nl, L, RP),
         out_shape=(
             jax.ShapeDtypeStruct((1, 3 * coeffs), F32),
             jax.ShapeDtypeStruct((1, R), F32),

time: 34.1 us -> 33.2 us (0.974)
  Pallas kernels: 33.3 us -> 32.4 us
    pallas_call x1, Pallas kernels: 31.8 us -> 30.9 us  [local(): pl.pallas_call(functools.partial(kernel, (W, S, nl, L, NTL, R)), out_shap...]
where the time goes in v3:
time: 33.2 us; the launch traced here: 33 us
  Pallas kernels  32.4 us (98%)
  between operations  0.64 us (2%)
    pallas_call x1, Pallas kernels, local(): pl.pallas_call(functools.partial(kernel, (W, S, nl, L, NTL, R)), out_shap...  30.9 us
    pallas_call x1, Pallas kernels, local(): pl.pallas_call(functools.partial(unfold, nl, L, RP), out_shape=(jax.Shape...  1.55 us

profile of v3, /device:TPU:0, one launch (start us, length us, event | category | flops | bytes accessed | tf_op | source)
XLA Modules:
  0.0 33.0 jit_solution(5249041140950974653)
XLA Ops:
  0.6 30.9 %shard_map.77 = (f32[2,72,128]{2,1,0:T(8,128)}, f32[1,64]{1,0:T(1,128)}) custom-call(bf16[64,8448]{1,0:T(8,128)(2,1)} %x_hbm.1, s32[1,64]{1,0:T(1,128)} %bitcast.4, f32[1,4224]{1,0:T(1,128)} %ctf_ref.1, bf16[1,8448]{1,0:T(2,128)(2,1)} %proj_ref.1, f32[4224]{0:T(1024)} %noise_ref.1, s32[2,32]{1,0:T(2,128)} %bitcast.3), custom_call_target="tpu_custom_call" | custom-call | tf_op jit(solution)/shard_map/pallas_call | solution.py:534
  31.5 1.5 %shard_map.78 = (f32[1,12672]{1,0:T(1,128)}, f32[1,64]{1,0:T(1,128)}) custom-call(f32[2,72,128]{2,1,0:T(8,128)} %get-tuple-element.6.rows_ref, f32[1,64]{1,0:T(1,128)} %get-tuple-element.7.ev_in), custom_call_target="tpu_custom_call" | custom-call | tf_op jit(solution)/shard_map/pallas_call | solution.py:586

commit v4 on v3

--- a/solution.py
+++ b/solution.py
@@ -82,7 +82,17 @@
     window = pl.ds(start, C)
 
     def chip_at(k):
-        return lax.rem(chip + k, NC)
+        if NC & (NC - 1):
+            return lax.rem(chip + k, NC)
+        other, bit = 0, 1
+        while bit < NC:
+            mine_bit = lax.rem(lax.div(chip, bit), 2)
+            other = other + bit * lax.rem(mine_bit + lax.rem(lax.div(k, bit), 2), 2)
+            bit *= 2
+        return other
+
+    def chip_from(k):
+        return lax.rem(chip + NC - k, NC) if NC & (NC - 1) else chip_at(k)
 
     def remote(src, dst, ssem, rsem, wide=None, shift=None):
         return pltpu.make_async_remote_copy(
@@ -151,7 +161,7 @@
         c.start()
 
     def ag_start(k, carry):
-        for c in ag_pair(chip_at(k) * 2 + core, ag_rsem.at[chip]):
+        for c in ag_pair(chip_at(NC - k) * 2 + core, ag_rsem.at[chip]):
             c.start()
         return carry
 
@@ -216,7 +226,7 @@
     square(w, 0)
 
     def relay(k, carry):
-        from_chip = lax.rem(chip + NC - k, NC)
+        from_chip = chip_from(k)
         settle(cbuf.at[:2], ag_rsem.at[from_chip])
         for c in relay_pair(from_chip * 2 + core):
             c.start()
@@ -293,8 +303,8 @@
         here = jnp.where(first + l >= s * L, 0.5, 0.0)
         wsq[:, cols] = curves * curves * noise * here
     p3, q3 = split3(power[...]), split3(wsq[...])
-    left = jnp.concatenate([p3[0], p3[0], p3[1], p3[1], p3[0], p3[2]], axis=1)
-    right = jnp.concatenate([q3[0], q3[1], q3[0], q3[1], q3[2], q3[0]], axis=1)
+    left = jnp.concatenate([p3[0], p3[0], p3[1]], axis=1)
+    right = jnp.concatenate([q3[0], q3[1], q3[0]], axis=1)
     self_g = dot(left, right, NT_DIMS)
     self_i = dot(jnp.concatenate(split3(self_g), axis=1), pick3)
     selfc[:H, :] = jnp.concatenate([self_i[:H], self_i[H:]], axis=1)
@@ -435,7 +445,7 @@
             snd[j, c * RP : (c + 1) * RP, :] = stage[at_row : at_row + RP, :].astype(BF16)
 
         def go(k, carry):
-            r2_copy(k, c).start()
+            r2_copy(NC - k, c).start()
             return carry
 
         lax.fori_loop(1, NC, go, 0)

time: 33.2 us -> 32.9 us (level)
  no operation moved by 1% of the time
where the time goes in v4:
time: 32.9 us; the launch traced here: 32.7 us
  Pallas kernels  32.1 us (98%)
  between operations  0.64 us (2%)
    pallas_call x1, Pallas kernels, local(): pl.pallas_call(functools.partial(kernel, (W, S, nl, L, NTL, R)), out_shap...  30.5 us
    pallas_call x1, Pallas kernels, local(): pl.pallas_call(functools.partial(unfold, nl, L, RP), out_shape=(jax.Shape...  1.55 us

profile of v4, /device:TPU:0, one launch (start us, length us, event | category | flops | bytes accessed | tf_op | source)
XLA Modules:
  0.0 32.7 jit_solution(17353354989155895832)
XLA Ops:
  0.6 30.5 %shard_map.77 = (f32[2,72,128]{2,1,0:T(8,128)}, f32[1,64]{1,0:T(1,128)}) custom-call(bf16[64,8448]{1,0:T(8,128)(2,1)} %x_hbm.1, s32[1,64]{1,0:T(1,128)} %bitcast.4, f32[1,4224]{1,0:T(1,128)} %ctf_ref.1, bf16[1,8448]{1,0:T(2,128)(2,1)} %proj_ref.1, f32[4224]{0:T(1024)} %noise_ref.1, s32[2,32]{1,0:T(2,128)} %bitcast.3), custom_call_target="tpu_custom_call" | custom-call | tf_op jit(solution)/shard_map/pallas_call | solution.py:544
  31.2 1.5 %shard_map.78 = (f32[1,12672]{1,0:T(1,128)}, f32[1,64]{1,0:T(1,128)}) custom-call(f32[2,72,128]{2,1,0:T(8,128)} %get-tuple-element.6.rows_ref, f32[1,64]{1,0:T(1,128)} %get-tuple-element.7.ev_in), custom_call_target="tpu_custom_call" | custom-call | tf_op jit(solution)/shard_map/pallas_call | solution.py:596
